TPU v7x, 512 devices: a whole 4x4x16 slice. The times are simulated.
512 devices in a mesh: leaf: 32 (over y, x, core), grp: 16 (over z).
Axes of the slice: x: 4, y: 4, z: 16, core: 2. Of those that a mesh axis runs over, the one named last changes fastest.
Arguments:
- rhs_local: float32 [32, 4, 1024, 128], P('leaf', None, 'grp'), may hold values from -6 to 6
- diag_inv_local: float32 [32, 4, 1024, 1024], P('leaf', None, 'grp'), may hold values from -0.1875 to 0.1875
- sub_local: float32 [32, 3, 1024, 1024], P('leaf', None, 'grp'), may hold values from -0.1875 to 0.1875
- tiles: float32 [32, 16, 3, 128, 1024], P('leaf', 'grp'), may hold values from -0.046875 to 0.046875
- tile_block: int32 [32, 16, 3], P('leaf', 'grp'), may hold values from 0 to 15
- tile_source: int32 [32, 16, 3], P('leaf', 'grp'), may hold values from 0 to 3
- tile_count: int32 [32, 16], P('leaf', 'grp'), may hold values from 1 to 3, as said below
- rhs_anc: float32 [2, 1024, 128], P(None, 'grp', 'leaf'), may hold values from -6 to 6
- diag_inv_anc: float32 [2, 1024, 1024], P(None, 'grp'), may hold values from -0.1875 to 0.1875
- sub_anc: float32 [1, 1024, 1024], P(None, 'grp'), may hold values from -0.1875 to 0.1875
Outputs:
- solution_local: float32 [32, 4, 1024, 128], P('leaf', None, 'grp')
- solution_anc: float32 [2, 1024, 128], P(None, 'grp', 'leaf')
Inputs may be any that keep to these rules, and one draw needn't show every extreme that they name: `tile_count`: some device holds exactly 3 live tiles.
All inputs are finite; a program needn't handle non-finite values.
Results may differ from a plain program's by a relative error of at most 0.0003.
Values sent between devices are 32-bit elements; how exact they have to be, the bound alone decides.
A program may use at most 64 MiB of HBM per device.

v0:
```python
import jax
import jax.numpy as jnp
from jax import lax
from jax.sharding import PartitionSpec as P

highest = lax.Precision.HIGHEST


def product(left, right):
    return jnp.dot(left, right, precision=highest, preferred_element_type=jnp.float32)


def fold_columns(matrix, portion):
    return product(matrix, portion)


def on_device(
    rhs_local,
    diag_inv_local,
    sub_local,
    tiles,
    tile_block,
    tile_source,
    tile_count,
    rhs_anc,
    diag_inv_anc,
    sub_anc,
):
    rhs_group = rhs_local[0]
    inverse_group = diag_inv_local[0]
    below_group = sub_local[0]
    supernodes = rhs_group.shape[0]
    block_order = inverse_group.shape[-1]
    rhs_count = rhs_group.shape[-1]
    solved = []
    gathered = []
    update = jnp.zeros_like(rhs_group[0])
    for current in range(supernodes):
        residual = rhs_group[current] - update
        owned = fold_columns(
            inverse_group[current], lax.all_gather(residual, "grp", axis=0, tiled=True)
        )
        solved.append(owned)
        full_solution = lax.all_gather(owned, "grp", axis=0, tiled=True)
        gathered.append(full_solution)
        if current + 1 < supernodes:
            update = product(below_group[current], full_solution)
    stacked = jnp.stack(gathered)
    tiles_mine = tiles[0, 0]
    blocks = tile_block[0, 0]
    sources = tile_source[0, 0]
    live_count = tile_count[0, 0]
    slots = tiles_mine.shape[0]
    tile_rows = tiles_mine.shape[1]
    ancestors = rhs_anc.shape[0]
    block_total = ancestors * block_order // tile_rows
    members = lax.axis_size("grp")
    owned_rows = block_order // members
    active = jnp.arange(slots, dtype=jnp.int32) < live_count
    chosen = stacked[sources]
    tile_terms = jnp.einsum(
        "mtk,mkr->mtr", tiles_mine, chosen, precision=highest, preferred_element_type=jnp.float32
    )
    onehot = (blocks[:, None] == jnp.arange(block_total, dtype=jnp.int32)[None, :]).astype(
        jnp.float32
    )
    onehot = onehot * active.astype(jnp.float32)[:, None]
    shaped = jnp.einsum(
        "mb,mtr->btr", onehot, tile_terms, precision=highest, preferred_element_type=jnp.float32
    ).reshape(ancestors, members, owned_rows, rhs_count)
    reduced = lax.psum_scatter(shaped, "grp", scatter_dimension=1, tiled=True)
    reduced = lax.psum_scatter(reduced, "leaf", scatter_dimension=3, tiled=True)
    part_mine = reduced[:, 0]
    ancestors_solved = []
    update = jnp.zeros_like(rhs_anc[0])
    for ancestor in range(ancestors):
        residual = rhs_anc[ancestor] - part_mine[ancestor] - update
        solution = fold_columns(
            diag_inv_anc[ancestor], lax.all_gather(residual, "grp", axis=0, tiled=True)
        )
        ancestors_solved.append(solution)
        if ancestor + 1 < ancestors:
            update = fold_columns(
                sub_anc[ancestor], lax.all_gather(solution, "grp", axis=0, tiled=True)
            )
    return (jnp.stack(solved)[None], jnp.stack(ancestors_solved))


def solution(mesh):
    return jax.shard_map(
        on_device,
        mesh=mesh,
        in_specs=(
            P("leaf", None, "grp", None),
            P("leaf", None, "grp", None),
            P("leaf", None, "grp", None),
            P("leaf", "grp", None, None, None),
            P("leaf", "grp", None),
            P("leaf", "grp", None),
            P("leaf", "grp"),
            P(None, "grp", "leaf"),
            P(None, "grp", None),
            P(None, "grp", None),
        ),
        out_specs=(P("leaf", None, "grp", None), P(None, "grp", "leaf")),
        check_vma=False,
    )
```

profile of v0, /device:TPU:6, one launch (start us, length us, event | category | flops | bytes accessed | tf_op | source)
XLA Modules:
  0.0 567.5 jit_solution(17628444517788647853)
XLA Ops:
  7.2 0.0 copy-start
  7.2 0.0 reduce-scatter.3.cloned.1.call-start
  7.2 0.9 slice.65
  8.2 38.9 %all-gather = f32[1,1,1024,128]{3,2,1,0:T(8,128)S(1)} all-gather(f32[1,1,64,128]{3,2,1,0:T(8,128)S(1)} %slice.65), channel_id=2, replica_groups=mesh['leaf'=32,'grp'=16] {'grp'}, dimensions={2}, use_global_device_ids=true | all-gather | bytes 557056 | tf_op jit(solution)/shard_map/all_gather | solution.py:41
  47.0 1.4 fusion.10
  48.4 29.2 %all_gather.34 = f32[1024,128]{1,0:T(8,128)S(1)} all-gather(f32[64,128]{1,0:T(8,128)S(1)} %fusion.10), channel_id=1, replica_groups=mesh['leaf'=32,'grp'=16] {'grp'}, dimensions={0}, use_global_device_ids=true | all-gather | bytes 557056 | tf_op jit(solution)/shard_map/all_gather | solution.py:44
  77.7 0.4 fusion.7
  78.1 31.1 %all_gather.35 = f32[1024,128]{1,0:T(8,128)S(1)} all-gather(f32[64,128]{1,0:T(8,128)S(1)} %fusion.7), channel_id=1, replica_groups=mesh['leaf'=32,'grp'=16] {'grp'}, dimensions={0}, use_global_device_ids=true | all-gather | bytes 557056 | tf_op jit(solution)/shard_map/all_gather | solution.py:41
  109.2 0.4 fusion.21
  109.6 29.1 %all_gather.36 = f32[1024,128]{1,0:T(8,128)S(1)} all-gather(f32[64,128]{1,0:T(8,128)S(1)} %bitcast.145), channel_id=1, replica_groups=mesh['leaf'=32,'grp'=16] {'grp'}, dimensions={0}, use_global_device_ids=true | all-gather | bytes 557056 | tf_op jit(solution)/shard_map/all_gather | solution.py:44
  138.8 0.4 fusion.6
  139.2 30.8 %all_gather.37 = f32[1024,128]{1,0:T(8,128)S(1)} all-gather(f32[64,128]{1,0:T(8,128)S(1)} %fusion.6), channel_id=1, replica_groups=mesh['leaf'=32,'grp'=16] {'grp'}, dimensions={0}, use_global_device_ids=true | all-gather | bytes 557056 | tf_op jit(solution)/shard_map/all_gather | solution.py:41
  170.1 0.4 fusion.18
  170.5 0.0 copy-start.8
  170.5 29.4 %all_gather.38 = f32[1024,128]{1,0:T(8,128)S(1)} all-gather(f32[64,128]{1,0:T(8,128)S(1)} %bitcast.147), channel_id=1, replica_groups=mesh['leaf'=32,'grp'=16] {'grp'}, dimensions={0}, use_global_device_ids=true | all-gather | bytes 557056 | tf_op jit(solution)/shard_map/all_gather | solution.py:44
  199.9 0.4 fusion.5
  200.3 30.6 %all_gather.39 = f32[1024,128]{1,0:T(8,128)S(1)} all-gather(f32[64,128]{1,0:T(8,128)S(1)} %fusion.5), channel_id=1, replica_groups=mesh['leaf'=32,'grp'=16] {'grp'}, dimensions={0}, use_global_device_ids=true | all-gather | bytes 557056 | tf_op jit(solution)/shard_map/all_gather | solution.py:41
  230.9 0.4 fusion.15
  231.4 28.8 %all_gather.40 = f32[1024,128]{1,0:T(8,128)S(1)} all-gather(f32[64,128]{1,0:T(8,128)S(1)} %bitcast.149), channel_id=1, replica_groups=mesh['leaf'=32,'grp'=16] {'grp'}, dimensions={0}, use_global_device_ids=true | all-gather | bytes 557056 | tf_op jit(solution)/shard_map/all_gather | solution.py:44
  260.2 1.5 pad_maximum_fusion
  261.7 2.2 gather_fusion
  264.0 0.0 copy-start.7
  264.0 2.6 fusion.2
  266.6 0.1 copy.18
  267.5 1.1 fusion.37
  268.6 0.3 copy.19
  269.0 0.0 copy-start.6
  269.0 0.0 copy-start.3
  269.0 1.1 copy.20
  270.1 0.0 reduce-scatter.3.cloned.1.call-update
  270.1 0.0 all-reduce.3.cloned.1.call-start
  270.1 68.0 %reduce-scatter.3.cloned.1.call-done = f32[2,1,64,128]{3,2,0,1:T(8,128)} async-done(((f32[2,16,64,128]{3,2,0,1:T(8,128)}), f32[2,1,64,128]{3,2,0,1:T(8,128)}) %reduce-scatter.3.cloned.1.call-update) | async-done | bytes 65552 | tf_op jit(solution)/shard_map/reduce_scatter | solution.py:71
  338.2 1.6 copy.21
  339.8 0.0 all-reduce.3.cloned.1.call-update
  339.8 0.7 maximum_bitcast_fusion
  340.4 1.3 dynamic-slice
  342.4 129.4 %all-reduce.3.cloned.1.call-done = f32[2,1,64,128]{2,3,1,0:T(8,128)} async-done(((f32[2,1,64,128]{2,3,1,0:T(8,128)}), f32[2,1,64,128]{2,3,1,0:T(8,128)}) %all-reduce.3.cloned.1.call-update) | async-done | bytes 65552
  471.8 0.7 fusion.36
  472.5 30.3 %all-gather.1 = f32[16,64,4]{1,2,0:T(4,128)S(1)} all-gather(f32[1,64,4]{1,2,0:T(4,128)S(1)} %fusion.36), channel_id=1, replica_groups=mesh['leaf'=32,'grp'=16] {'grp'}, dimensions={0}, use_global_device_ids=true | all-gather | bytes 17408 | tf_op jit(solution)/shard_map/all_gather | solution.py:79
  502.8 0.1 reshape.78
  502.9 0.3 convolution_bitcast_fusion.5
  503.1 27.5 %all-gather.2 = f32[16,64,4]{1,2,0:T(4,128)S(1)} all-gather(f32[1,64,4]{1,2,0:T(4,128)S(1)} %convolution_bitcast_fusion.5), channel_id=1, replica_groups=mesh['leaf'=32,'grp'=16] {'grp'}, dimensions={0}, use_global_device_ids=true | all-gather | bytes 17408 | tf_op jit(solution)/shard_map/all_gather | solution.py:84
  530.6 0.1 reshape.80
  530.7 1.0 fusion.9
  531.7 28.0 %all-gather.3 = f32[16,64,4]{1,2,0:T(4,128)S(1)} all-gather(f32[1,64,4]{1,2,0:T(4,128)S(1)} %fusion.9), channel_id=1, replica_groups=mesh['leaf'=32,'grp'=16] {'grp'}, dimensions={0}, use_global_device_ids=true | all-gather | bytes 17408 | tf_op jit(solution)/shard_map/all_gather | solution.py:79
  559.6 0.1 reshape.82
  559.7 0.3 convolution_bitcast_fusion.3
  560.0 0.7 pad_maximum_fusion.1
  (19 shorter events, 0.1 us)
Async XLA Ops:
  7.2 256.8 %copy-start = (f32[1,1,3,128,1024]{4,3,2,1,0:T(8,128)S(1)}, f32[1,1,3,128,1024]{4,3,2,1,0:T(8,128)}, u32[]{:S(2)}) copy-start(f32[1,1,3,128,1024]{4,3,2,1,0:T(8,128)} %param.13) | copy-start | bytes 4718596
  7.2 70.5 %copy-start.5 = (f32[1,4,64,128]{3,2,1,0:T(8,128)S(1)}, f32[1,4,64,128]{3,2,1,0:T(8,128)}, u32[]{:S(2)}) copy-start(f32[1,4,64,128]{3,2,1,0:T(8,128)} %param.10) | copy-start | bytes 393220
  7.2 70.5 %copy-start.2 = (f32[1,3,64,1024]{3,2,1,0:T(8,128)S(1)}, f32[1,3,64,1024]{3,2,1,0:T(8,128)}, u32[]{:S(2)}) copy-start(f32[1,3,64,1024]{3,2,1,0:T(8,128)} %param.12) | copy-start | bytes 2359300
  7.2 331.0 %reduce-scatter.3.cloned.1.call-start = ((), (), s32[]{:S(2)}) async-start(), calls=%async_computation.1 | async-start | bytes 1114112 | tf_op jit(solution)/shard_map/reduce_scatter | solution.py:71
  8.2 101.0 %copy-start.1 = (f32[1,4,64,1024]{3,2,1,0:T(8,128)S(1)}, f32[1,4,64,1024]{3,2,1,0:T(8,128)}, u32[]{:S(2)}) copy-start(f32[1,4,64,1024]{3,2,1,0:T(8,128)} %param.11) | copy-start | bytes 3145732
  170.5 89.7 %copy-start.8 = (s32[1,1,3]{2,1,0:T(1,128)S(1)}, s32[1,1,3]{2,1,0:T(1,128)}, u32[]{:S(2)}) copy-start(s32[1,1,3]{2,1,0:T(1,128)} %param.15) | copy-start | bytes 40
  264.0 3.5 copy-start.7
  269.0 202.8 %copy-start.6 = (f32[2,64,4]{1,2,0:T(4,128)S(1)}, f32[2,64,4]{1,2,0:T(4,128)}, u32[]{:S(2)}) copy-start(f32[2,64,4]{1,2,0:T(4,128)} %param.17) | copy-start | bytes 6148
  269.0 233.9 %copy-start.3 = (f32[2,64,1024]{2,1,0:T(8,128)S(1)}, f32[2,64,1024]{2,1,0:T(8,128)}, u32[]{:S(2)}) copy-start(f32[2,64,1024]{2,1,0:T(8,128)} %param.18) | copy-start | bytes 1572868
  270.1 260.7 %copy-start.4 = (f32[1,64,1024]{2,1,0:T(8,128)S(1)}, f32[1,64,1024]{2,1,0:T(8,128)}, u32[]{:S(2)}) copy-start(f32[1,64,1024]{2,1,0:T(8,128)} %param.19) | copy-start | bytes 786436
  270.1 201.7 %all-reduce.3.cloned.1.call-start = ((), (), s32[]{:S(2)}) async-start(), calls=%async_computation.2 | async-start | bytes 262144
Sparse Core Ops, SparseCore 0:
  270.2 67.9 reduce-scatter.2
  341.4 130.3 all-reduce.2
where the time goes:
time: 568 us; the launch traced here: 567 us
  blocking collectives  334 us (59%)
  waiting for transfers between devices  197 us (35%)
  between operations  15.5 us (3%)
  matrix products  9.31 us (2%)
  local copies, waits for them, and re-layouts  7.88 us (1%)
    all_gather x6, blocking collectives, on_device(): lax.all_gather(residual, 'grp', axis=0, tiled=True)  190 us
    unnamed x3, waiting for transfers between devices  129 us
    all_gather x4, blocking collectives, on_device(): full_solution = lax.all_gather(owned, 'grp', axis=0, tiled=True)  117 us
    reduce_scatter x1, waiting for transfers between devices, on_device(): reduced = lax.psum_scatter(shaped, 'grp', scatter_dimension=1, tiled=True)  68 us
    all_gather x1, blocking collectives, on_device(): lax.all_gather(solution, 'grp', axis=0, tiled=True)  27.5 us
  transfers between devices with their start and end apart: 2, of which 2 were waited for; matrix products, arithmetic and copies ran while one was open for 0% of the time, Pallas kernels for 0%

commit v1 on v0

v1 whole, which is shorter than its diff:
```python
import jax
import jax.numpy as jnp
from jax import lax
from jax.experimental import pallas as pl
from jax.experimental.pallas import tpu as pltpu
from jax.sharding import PartitionSpec as P

HI = lax.Precision.HIGHEST
F32 = jnp.float32
N = 16
SIDE = 4
CHAIN = 4
ROWS = 64
RHS = 128
TILES = 3
SLOTS = 9

CHILDREN = {0: (3, 1), 3: (6, 4, 2), 6: (8, 7, 5)}
ORDER = (1, 3, 2, 4, 6, 5, 7, 8)
EDGES = sorted({abs(b - a) for a, bs in CHILDREN.items() for b in bs})


def dot(a, b):
    return jnp.dot(a, b, precision=HI, preferred_element_type=F32)


def dot_nt(a, b):
    return lax.dot_general(a, b, (((1,), (1,)), ((), ())), precision=HI, preferred_element_type=F32)


def kernel(
    block_s, source_s, count_s, rhs, rhs_anc, dinv_h, sub_h, tiles_h, dinva_h, suba_h,
    out_local, out_anc,
    dinv, sub, tiles, dinva, suba,
    pd, pt, gr, gx, gl, gz, old, cells, pool, theirs, inbox1, mid, inbox2, zbuf, ebuf, fbuf, relmat, give, take, prow,
    load_sem, send_sem, recv_sem, pair_send, pair_recv, one_send, one_recv, two_send, two_recv,
    e_send, e_recv, f_send, f_recv, last_send, last_recv,
):
    me = lax.axis_index("grp")
    leaf = lax.axis_index("leaf")
    core = lax.rem(leaf, 2)
    x = lax.rem(lax.div(leaf, 2), SIDE)
    y = lax.div(leaf, 2 * SIDE)
    partner = leaf + 1 - 2 * core
    p_one = jnp.where(core == 0, x, y)
    p_two = jnp.where(core == 0, y, x)

    def leaf_of(one, two):
        xx = jnp.where(core == 0, one, two)
        yy = jnp.where(core == 0, two, one)
        return (yy * SIDE + xx) * 2 + core

    def z_at(step):
        return lax.rem(me + (step + 2 * N), N)

    one_of = [leaf_of(lax.rem(p_one + d, SIDE), p_two) for d in range(SIDE)]
    two_of = [leaf_of(p_one, lax.rem(p_two + d, SIDE)) for d in range(SIDE)]

    loads = [
        pltpu.make_async_copy(src, dst, load_sem.at[i])
        for i, (src, dst) in enumerate(
            ((dinv_h.at[0], dinv), (sub_h.at[0], sub), (tiles_h.at[0, 0], tiles), (dinva_h, dinva), (suba_h, suba))
        )
    ]
    for load in loads:
        load.start()

    prow[...] = jnp.zeros_like(prow)
    ebuf[0] = jnp.zeros((8, 128), F32)
    give[2] = jnp.zeros((8, 128), F32)
    take[0] = jnp.zeros((8, 128), F32)
    barrier = pltpu.get_barrier_semaphore()
    greeted = 0
    for step in EDGES:
        for sign in (1, -1):
            pl.semaphore_signal(barrier, inc=1, device_id={"grp": z_at(sign * step)}, device_id_type=pl.DeviceIdType.MESH)
            greeted += 1
    for other in (partner, *one_of[1:], *two_of[1:]):
        pl.semaphore_signal(barrier, inc=1, device_id={"leaf": other}, device_id_type=pl.DeviceIdType.MESH)
        greeted += 1
    pl.semaphore_wait(barrier, greeted)

    def buffer(k):
        if k == 8:
            return gz
        if k == 7:
            return gl
        return gr.at[k // 2] if k % 2 == 0 else gx.at[k // 2]

    def view(k, d, b):
        buf = buffer(k)
        if b == 0:
            return rhs.at[0, 0] if k == 0 else buf.at[0, 0:ROWS]
        if b == 8:
            return buf.at[0, ROWS + 32 * d : ROWS + 32 * d + 32]
        return buf.at[b, ROWS * d : ROWS * d + ROWS]

    def edge(k, d, a, b):
        src = view(k, d, a)
        if b == 8:
            src = src.at[32 * d : 32 * d + 32]
        step = b - a if d == 0 else a - b
        return pltpu.make_async_remote_copy(
            src_ref=src,
            dst_ref=view(k, d, b),
            send_sem=send_sem.at[k, d, b - 1],
            recv_sem=recv_sem.at[k, d, b - 1],
            device_id={"grp": z_at(step)},
            device_id_type=pl.DeviceIdType.MESH,
        )

    parent = {b: a for a, bs in CHILDREN.items() for b in bs}

    def gather(k, consume, between=None):
        for b in CHILDREN[0]:
            for d in (0, 1):
                edge(k, d, 0, b).start()
        if between is not None:
            between(0)
        consume(0)
        for place, b in enumerate(ORDER):
            for d in (0, 1):
                edge(k, d, parent[b], b).wait_recv()
                for c in CHILDREN.get(b, ()):
                    edge(k, d, b, c).start()
            consume(b)
            if between is not None:
                between(place + 1)

    def finish(k):
        for b in range(1, 9):
            for d in (0, 1):
                edge(k, d, parent[b], b).wait_send()

    shift = lax.rem((N - me) * ROWS, N * ROWS)

    def turned(matrix):
        return pltpu.roll(matrix, shift, axis=1)

    def paired(matrix, j):
        if j == 0:
            return matrix[:, 0:ROWS]
        if j == 8:
            return matrix[:, 8 * ROWS : 9 * ROWS]
        return jnp.concatenate(
            [matrix[:, (N - j) * ROWS : (N - j + 1) * ROWS], matrix[:, j * ROWS : (j + 1) * ROWS]], axis=1
        )

    def prepare(i):
        matrix = turned(dinv[i // 2] if i % 2 == 0 else sub[i // 2])
        for j in range(SLOTS):
            piece = paired(matrix, j)
            pd[i, j, :, 0 : piece.shape[1]] = piece

    def prepare_tile(m):
        matrix = turned(tiles[m])
        for j in range(SLOTS):
            piece = paired(matrix, j)
            pt[j, m * 128 : (m + 1) * 128, 0 : piece.shape[1]] = piece

    def chunk(buf, j):
        if j == 0:
            return buf[0, 0:ROWS]
        if j == 8:
            return buf[0, ROWS : 2 * ROWS]
        return buf[j]

    def multiply(i, k):
        total = []
        buf = buffer(k)

        def consume(b):
            left = pd[i, b, :, 0:ROWS] if b in (0, 8) else pd[i, b]
            right = rhs[0, 0] if (k == 0 and b == 0) else chunk(buf, b)
            term = dot(left, right)
            if total:
                total[0] = total[0] + term
            else:
                total.append(term)

        return total, consume

    sources = [source_s[0, 0, m] for m in range(TILES)]
    blocks = [block_s[0, 0, m] for m in range(TILES)]
    live = count_s[0, 0]

    def earlier(b):
        for m in range(TILES):
            rows = slice(m * 128, (m + 1) * 128)
            left = pt[b, rows, 0:ROWS] if b in (0, 8) else pt[b, rows]
            at = jnp.minimum(sources[m], CHAIN - 2)
            if b == 0:
                right = gx[at, 0, 0:ROWS]
            elif b == 8:
                right = gx[at, 0, ROWS : 2 * ROWS]
            else:
                right = gx[at, b]
            term = dot(left, right)
            if b == 0:
                old[m] = term
            else:
                old[m] += term

    loads[0].wait()
    loads[1].wait()
    for s in range(CHAIN):
        k = 2 * s
        total, consume = multiply(k, k)
        if s == 0:

            def between(step):
                if step == 0:
                    prepare(0)
                elif step < 7:
                    prepare(step)

        elif s == 1:

            def between(step):
                if step == 0:
                    loads[2].wait()
                    loads[3].wait()
                    loads[4].wait()
                elif step <= TILES:
                    prepare_tile(step - 1)
                elif step == 4:
                    relmat[0] = turned(suba[0])
                elif step == 5:
                    relmat[1] = turned(dinva[1])

        elif s == 2:
            between = None
        else:

            def between(step):
                earlier(0 if step == 0 else ORDER[step - 1])

        gather(k, consume, between)
        solved = total[0]
        buffer(k + 1)[0, 0:ROWS] = solved
        out_local[0, s] = solved
        if s + 1 < CHAIN:
            total, consume = multiply(k + 1, k + 1)
            gather(k + 1, consume)
            buffer(k + 2)[0, 0:ROWS] = rhs[0, s + 1] - total[0]
    for m in range(TILES):
        old[m] = jnp.where(sources[m] == CHAIN - 1, 0.0, old[m])

    last = []

    def consume_last(b):
        left = pt[b, :, 0:ROWS] if b in (0, 8) else pt[b]
        term = dot(left, chunk(gl, b))
        if last:
            last[0] = last[0] + term
        else:
            last.append(term)

    gather(7, consume_last)
    for m in range(TILES):
        term = jnp.where(sources[m] == CHAIN - 1, last[0][m * 128 : (m + 1) * 128], old[m])
        term = jnp.where(m < live, term, 0.0)
        cells[m] = jnp.transpose(term).reshape(N, 8, 128)

    half = lax.rem(me, 2)
    home = lax.div(me, 2)
    lane = lax.broadcasted_iota(jnp.int32, (8, 128), 1)
    sub_at = lax.broadcasted_iota(jnp.int32, (8, 128), 0)
    inside = jnp.logical_and(lax.div(lane, ROWS) == half, lax.div(sub_at, 4) == core)
    for a in range(2):
        prow[0:ROWS, 0:4] = rhs_anc[a]
        tall = jnp.transpose(prow[...])
        quad = tall[0:8]
        wide = jnp.where(sub_at < 4, quad, pltpu.roll(quad, 4, axis=0))
        wide = jnp.where(lane < ROWS, wide, pltpu.roll(wide, ROWS, axis=1))
        give[a] = jnp.where(inside, wide, 0.0)

    def build(role, out):
        for d in range(SIDE):
            for e in range(SIDE):
                xx = jnp.where(role == 0, lax.rem(x + d, SIDE), lax.rem(x + e, SIDE))
                yy = jnp.where(role == 0, lax.rem(y + e, SIDE), lax.rem(y + d, SIDE))
                cell = yy * SIDE + xx
                pieces = [cells[m, cell] for m in range(TILES)]
                for b in range(8):
                    value = jnp.zeros((8, 128), F32)
                    for m in range(TILES):
                        value = value - jnp.where(blocks[m] == role * 8 + b, pieces[m], 0.0)
                    if d == 0 and e == 0:
                        value = value + jnp.where(home == b, give[role], 0.0)
                    out[d, e, b] = value

    def remote(src, dst, send, recv, **where):
        return pltpu.make_async_remote_copy(
            src_ref=src, dst_ref=dst, send_sem=send, recv_sem=recv, device_id=where, device_id_type=pl.DeviceIdType.MESH
        )

    build(1 - core, theirs)
    pairs = [remote(theirs.at[d], pool.at[d], pair_send.at[d], pair_recv.at[d], leaf=partner) for d in range(SIDE)]
    for d in (2, 1, 3, 0):
        pairs[d].start()
    build(core, mid)
    ones = [None] + [
        remote(mid.at[d], inbox1.at[d - 1], one_send.at[d - 1], one_recv.at[d - 1], leaf=one_of[d]) for d in range(1, SIDE)
    ]
    for d in (2, 1, 3, 0):
        pairs[d].wait_recv()
        mid[d] = mid[d] + pool[d]
        if d:
            ones[d].start()
    for d in (1, 3, 2):
        ones[d].wait_recv()
    zbuf[...] = mid[0] + inbox1[0] + inbox1[1] + inbox1[2]
    twos = [None] + [
        remote(zbuf.at[d], inbox2.at[d - 1], two_send.at[d - 1], two_recv.at[d - 1], leaf=two_of[d]) for d in range(1, SIDE)
    ]
    for d in (2, 1, 3):
        twos[d].start()
    for d in (1, 3, 2):
        twos[d].wait_recv()
    gz[0, 0:ROWS] = (zbuf[0] + inbox2[0] + inbox2[1] + inbox2[2]).reshape(ROWS, RHS)

    sums = []

    def add_up(b):
        piece = chunk(gz, b)
        if b not in (0, 8):
            piece = piece[0:ROWS] + piece[ROWS : 2 * ROWS]
        if sums:
            sums[0] = sums[0] + piece
        else:
            sums.append(piece)

    gather(8, add_up)
    wanted = sums[0]
    first = jnp.zeros((8, ROWS), F32)
    for b in range(8):
        first = first + dot_nt(wanted[b * 8 : b * 8 + 8], dinva[core, :, b * 128 : (b + 1) * 128])

    def row_of(buf):
        return jnp.concatenate([buf[(N - r) % N, :, 0:ROWS] for r in range(N)], axis=1)

    ebuf[0, :, 0:ROWS] = first

    def e_copy(t):
        return remote(ebuf.at[0], ebuf.at[t], e_send.at[t], e_recv.at[t], grp=z_at(t))

    def f_copy(t):
        there = {"leaf": partner} if t == 0 else {"leaf": partner, "grp": z_at(t)}
        return remote(give.at[2], fbuf.at[t], f_send.at[t], f_recv.at[t], **there)

    def swap():
        return remote(take.at[0], take.at[1], last_send.at[0], last_recv.at[0], leaf=partner)

    order = sorted(range(1, N), key=lambda t: -min(t, N - t))

    @pl.when(core == 0)
    def _():
        for t in order:
            e_copy(t).start()
        take[0, :, 0:ROWS] = ebuf[0, :, 0:ROWS]
        swap().start()
        for t in reversed(order):
            e_copy(t).wait_recv()
        give[2, :, 0:ROWS] = dot_nt(row_of(ebuf), relmat[0])
        for t in order:
            f_copy(t).start()
        f_copy(0).start()
        for t in range(N):
            f_copy(t).wait_send()
        for t in order:
            e_copy(t).wait_send()

    @pl.when(core == 1)
    def _():
        for t in [0, *reversed(order)]:
            f_copy(t).wait_recv()
        take[0, :, 0:ROWS] = ebuf[0, :, 0:ROWS] - dot_nt(row_of(fbuf), relmat[1])
        swap().start()

    swap().wait_recv()
    for a in range(2):
        kept = jnp.where(core == a, take[0], take[1])
        kept = jnp.where(core == 0, kept, pltpu.roll(kept, 4, axis=0))
        prow[0:8, :] = kept
        tall = jnp.transpose(prow[...])
        out_anc[a] = tall[0:ROWS, 0:4]

    swap().wait_send()
    for k in range(9):
        finish(k)
    for d in range(SIDE):
        pairs[d].wait_send()
        if d:
            ones[d].wait_send()
            twos[d].wait_send()


def on_device(rhs_local, diag_inv_local, sub_local, tiles, tile_block, tile_source, tile_count, rhs_anc, diag_inv_anc, sub_anc):
    vmem = pl.BlockSpec(memory_space=pltpu.VMEM)
    smem = pl.BlockSpec(memory_space=pltpu.SMEM)
    hbm = pl.BlockSpec(memory_space=pl.ANY)
    dma = pltpu.SemaphoreType.DMA
    return pl.pallas_call(
        kernel,
        out_shape=(
            jax.ShapeDtypeStruct((1, CHAIN, ROWS, RHS), F32),
            jax.ShapeDtypeStruct((2, ROWS, 4), F32),
        ),
        in_specs=[smem, smem, smem, vmem, vmem, hbm, hbm, hbm, hbm, hbm],
        out_specs=(vmem, vmem),
        scratch_shapes=[
            pltpu.VMEM((4, ROWS, 1024), F32),
            pltpu.VMEM((3, ROWS, 1024), F32),
            pltpu.VMEM((TILES, 128, 1024), F32),
            pltpu.VMEM((2, ROWS, 1024), F32),
            pltpu.VMEM((1, ROWS, 1024), F32),
            pltpu.VMEM((7, SLOTS, ROWS, 128), F32),
            pltpu.VMEM((SLOTS, TILES * 128, 128), F32),
            pltpu.VMEM((4, 8, 128, RHS), F32),
            pltpu.VMEM((3, 8, 128, RHS), F32),
            pltpu.VMEM((8, 128, RHS), F32),
            pltpu.VMEM((8, 128, RHS), F32),
            pltpu.VMEM((TILES, 128, RHS), F32),
            pltpu.VMEM((TILES, N, 8, 128), F32),
            pltpu.VMEM((SIDE, SIDE, 8, 8, 128), F32),
            pltpu.VMEM((SIDE, SIDE, 8, 8, 128), F32),
            pltpu.VMEM((3, SIDE, 8, 8, 128), F32),
            pltpu.VMEM((SIDE, SIDE, 8, 8, 128), F32),
            pltpu.VMEM((3, 8, 8, 128), F32),
            pltpu.VMEM((SIDE, 8, 8, 128), F32),
            pltpu.VMEM((N, 8, 128), F32),
            pltpu.VMEM((N, 8, 128), F32),
            pltpu.VMEM((2, ROWS, 1024), F32),
            pltpu.VMEM((3, 8, 128), F32),
            pltpu.VMEM((2, 8, 128), F32),
            pltpu.VMEM((128, 128), F32),
            dma((5,)),
            dma((9, 2, 8)),
            dma((9, 2, 8)),
            dma((SIDE,)),
            dma((SIDE,)),
            dma((3,)),
            dma((3,)),
            dma((3,)),
            dma((3,)),
            dma((N,)),
            dma((N,)),
            dma((N,)),
            dma((N,)),
            dma((1,)),
            dma((1,)),
        ],
        compiler_params=pltpu.CompilerParams(
            collective_id=0, has_side_effects=True, vmem_limit_bytes=56 * 1024 * 1024
        ),
    )(tile_block, tile_source, tile_count, rhs_local, rhs_anc, diag_inv_local, sub_local, tiles, diag_inv_anc, sub_anc)


def solution(mesh):
    return jax.shard_map(
        on_device,
        mesh=mesh,
        in_specs=(
            P("leaf", None, "grp", None),
            P("leaf", None, "grp", None),
            P("leaf", None, "grp", None),
            P("leaf", "grp", None, None, None),
            P("leaf", "grp", None),
            P("leaf", "grp", None),
            P("leaf", "grp"),
            P(None, "grp", "leaf"),
            P(None, "grp", None),
            P(None, "grp", None),
        ),
        out_specs=(P("leaf", None, "grp", None), P(None, "grp", "leaf")),
        check_vma=False,
    )
```

time: 568 us -> 195 us (0.34)
  blocking collectives: 334 us -> 0 us
  waiting for transfers between devices: 197 us -> 0 us
  Pallas kernels: 0 us -> 186 us
  between operations: 15.5 us -> 1.29 us
  matrix products: 9.31 us -> 0 us
    all_gather x11 -> x0, blocking collectives: 334 us -> none  [the longest x6 190 us: on_device(): lax.all_gather(residual, 'grp', axis=0, tiled=True)]
    pallas_call x0 -> x1, Pallas kernels: none -> 186 us  [on_device(): pl.pallas_call(kernel, out_shape=(jax.ShapeDtypeStruct((1, CHAIN, ROWS, R...]
    unnamed x3 -> x0, waiting for transfers between devices: 129 us -> none
    reduce_scatter x1 -> x0, waiting for transfers between devices: 68 us -> none  [on_device(): reduced = lax.psum_scatter(shaped, 'grp', scatter_dimension=1, tiled=True)]
    dot_general x12 -> x0, matrix products: 9.31 us -> none  [the longest x10 5.54 us: product(): jnp.dot(left, right, precision=highest, preferred_element_type=jnp.float32)]
  transfers between devices with their start and end apart: 2 -> 0, of which waited for: 2 -> 0; matrix products, arithmetic and copies ran while one was open for 0% -> 0% of each run, Pallas kernels for 0% -> 0%
where the time goes in v1:
time: 195 us; the launch traced here: 191 us
  Pallas kernels  186 us (95%)
  local copies, waits for them, and re-layouts  4.5 us (2%)
    pallas_call x1, Pallas kernels, on_device(): pl.pallas_call(kernel, out_shape=(jax.ShapeDtypeStruct((1, CHAIN, ROWS, R...  186 us

profile of v1, /device:TPU:6, one launch (start us, length us, event | category | flops | bytes accessed | tf_op | source)
XLA Modules:
  0.0 191.5 jit_solution(1206127002373581991)
XLA Ops:
  1.3 1.4 copy.12.rhs_anc
  2.7 185.7 %shard_map.113 = (f32[1,4,64,128]{3,2,1,0:T(8,128)}, f32[2,64,4]{2,1,0:T(8,128)}) custom-call(s32[1,1,3]{2,1,0:T(1,128)} %block_s.1, s32[1,1,3]{2,1,0:T(1,128)} %source_s.1, s32[1,1]{1,0:T(1,128)S(6)} %copy.15.count_s, f32[1,4,64,128]{3,2,1,0:T(8,128)} %rhs.1, f32[2,64,4]{2,1,0:T(8,128)} %copy.12.rhs_anc, f32[1,4,64,1024]{3,2,1,0:T(8,128)} %dinv_h.1, ...), custom_call_target="tpu_custom_call" | custom-call | tf_op jit(solution)/shard_map/pallas_call | solution.py:404
  188.4 1.5 copy.13
  189.9 1.6 copy.16

commit v2 on v1

v2 whole, which is shorter than its diff:
```python
import jax
import jax.numpy as jnp
from jax import lax
from jax.experimental import pallas as pl
from jax.experimental.pallas import tpu as pltpu
from jax.sharding import PartitionSpec as P

HI = lax.Precision.HIGHEST
F32 = jnp.float32
N = 16
SIDE = 4
CHAIN = 4
ROWS = 64
RHS = 128
TILES = 3
SLOTS = 9

CHILDREN = {0: (5, 2, 1), 2: (3,), 5: (8, 7, 6, 4)}
RELAYS = ((5, 2),)
EARLY = (1, 2, 5)
LATE = (3, 6, 4, 7, 8)
RING = {i: (i + 1,) for i in range(8)}
PIECES = 2
EDGES = sorted({abs(b - a) for tree in (CHILDREN, RING) for a, bs in tree.items() for b in bs})


def dot(a, b):
    return jnp.dot(a, b, precision=HI, preferred_element_type=F32)


def dot_nt(a, b):
    return lax.dot_general(a, b, (((1,), (1,)), ((), ())), precision=HI, preferred_element_type=F32)


def kernel(
    block_s, source_s, count_s, rhs, rhs_anc, dinv_h, sub_h, tiles_h, dinva_h, suba_h,
    out_local, out_anc,
    dinv, sub, tiles, dinva, suba,
    pd, pt, gr, gx, gl, gz, old, cells, pool, theirs, inbox1, mid, inbox2, zbuf, gb, tacc, tfull, wfull, give, swap_out, swap_in, prow,
    load_sem, send_sem, recv_sem, pair_send, pair_recv, one_send, one_recv, two_send, two_recv,
    t_send, t_recv, w_send, w_recv, swap_send, swap_recv,
):
    me = lax.axis_index("grp")
    leaf = lax.axis_index("leaf")
    core = lax.rem(leaf, 2)
    x = lax.rem(lax.div(leaf, 2), SIDE)
    y = lax.div(leaf, 2 * SIDE)
    partner = leaf + 1 - 2 * core
    p_one = jnp.where(core == 0, x, y)
    p_two = jnp.where(core == 0, y, x)

    def leaf_of(one, two):
        xx = jnp.where(core == 0, one, two)
        yy = jnp.where(core == 0, two, one)
        return (yy * SIDE + xx) * 2 + core

    def z_at(step):
        return lax.rem(me + (step + 2 * N), N)

    one_of = [leaf_of(lax.rem(p_one + d, SIDE), p_two) for d in range(SIDE)]
    two_of = [leaf_of(p_one, lax.rem(p_two + d, SIDE)) for d in range(SIDE)]

    loads = [
        pltpu.make_async_copy(src, dst, load_sem.at[i])
        for i, (src, dst) in enumerate(
            ((dinv_h.at[0], dinv), (sub_h.at[0], sub), (tiles_h.at[0, 0], tiles), (dinva_h, dinva), (suba_h, suba))
        )
    ]
    for load in loads:
        load.start()

    prow[...] = jnp.zeros_like(prow)
    swap_out[...] = jnp.zeros_like(swap_out)
    barrier = pltpu.get_barrier_semaphore()
    greeted = 0
    for step in EDGES:
        for sign in (1, -1):
            pl.semaphore_signal(barrier, inc=1, device_id={"grp": z_at(sign * step)}, device_id_type=pl.DeviceIdType.MESH)
            greeted += 1
    near = [((lax.div(y, 2) * 2 + dy) * SIDE + dx) * 2 + 1 - core for dy in range(2) for dx in range(SIDE)]
    for other in (*near, *one_of[1:], *two_of[1:]):
        pl.semaphore_signal(barrier, inc=1, device_id={"leaf": other}, device_id_type=pl.DeviceIdType.MESH)
        greeted += 1
    pl.semaphore_wait(barrier, greeted)

    def buffer(k):
        if k == 9:
            return gb
        if k == 8:
            return gz
        if k == 7:
            return gl
        return gr.at[k // 2] if k % 2 == 0 else gx.at[k // 2]

    part = ROWS // PIECES

    def view(k, d, b, p):
        buf = buffer(k)
        if b == 0:
            return rhs.at[0, 0, p * part : (p + 1) * part] if k == 0 else buf.at[0, p * part : (p + 1) * part]
        base = ROWS if b == 8 else ROWS * d
        return buf.at[b % 8, base + p * part : base + (p + 1) * part]

    def ways(b, p):
        return (0, 1) if b < 8 else (2 * p // PIECES,)

    def edge(k, d, a, b, p):
        step = b - a if d == 0 else a - b
        return pltpu.make_async_remote_copy(
            src_ref=view(k, d, a, p),
            dst_ref=view(k, d, b, p),
            send_sem=send_sem.at[k, d, b - 1, p],
            recv_sem=recv_sem.at[k, d, b - 1, p],
            device_id={"grp": z_at(step)},
            device_id_type=pl.DeviceIdType.MESH,
        )

    def tree(k):
        return RING if k == 9 else CHILDREN

    parents = {k: {b: a for a, bs in tree(k).items() for b in bs} for k in range(10)}

    def send_own(k):
        for b in tree(k)[0]:
            for p in range(PIECES):
                for d in ways(b, p):
                    edge(k, d, 0, b, p).start()

    def receive(k, b):
        for p in range(PIECES):
            for d in ways(b, p):
                edge(k, d, parents[k][b], b, p).wait_recv()

    def pass_on(k, relays):
        for p in range(PIECES):
            for b in relays:
                for d in ways(b, p):
                    edge(k, d, parents[k][b], b, p).wait_recv()
                for c in tree(k)[b]:
                    for d in ways(c, p):
                        edge(k, d, b, c, p).start()

    def gather(k, consume, first=None, second=None):
        send_own(k)
        if first is not None:
            first()
        consume(0)
        relays = [b for phase in RELAYS for b in phase]
        pass_on(k, RELAYS[0])
        for b in EARLY:
            if b not in relays:
                receive(k, b)
            consume(b)
        for phase in RELAYS[1:]:
            pass_on(k, phase)
            for b in phase:
                consume(b)
        if second is not None:
            second()
        for b in LATE:
            receive(k, b)
            consume(b)

    def finish(k):
        for b, a in parents[k].items():
            for p in range(PIECES):
                for d in ways(b, p):
                    edge(k, d, a, b, p).wait_send()

    shift = lax.rem((N - me) * ROWS, N * ROWS)

    def turned(matrix):
        return pltpu.roll(matrix, shift, axis=1)

    def paired(matrix, j):
        if j == 0:
            return matrix[:, 0:ROWS]
        if j == 8:
            return matrix[:, 8 * ROWS : 9 * ROWS]
        return jnp.concatenate(
            [matrix[:, (N - j) * ROWS : (N - j + 1) * ROWS], matrix[:, j * ROWS : (j + 1) * ROWS]], axis=1
        )

    def store_pairs(i, matrix):
        for j in range(SLOTS):
            piece = paired(matrix, j)
            pd[i, j, :, 0 : piece.shape[1]] = piece

    def prepare(*which):
        for i in which:
            store_pairs(i, turned(dinv[i // 2] if i % 2 == 0 else sub[i // 2]))

    def prepare_tile(m):
        matrix = turned(tiles[m])
        for j in range(SLOTS):
            piece = paired(matrix, j)
            pt[j, m * 128 : (m + 1) * 128, 0 : piece.shape[1]] = piece

    def chunk(buf, j):
        if j == 0:
            return buf[0, 0:ROWS]
        if j == 8:
            return buf[0, ROWS : 2 * ROWS]
        return buf[j]

    def multiply(i, k):
        total = []
        buf = buffer(k)

        def consume(b):
            left = pd[i, b, :, 0:ROWS] if b in (0, 8) else pd[i, b]
            right = rhs[0, 0] if (k == 0 and b == 0) else chunk(buf, b)
            term = dot(left, right)
            if total:
                total[0] = total[0] + term
            else:
                total.append(term)

        return total, consume

    sources = [source_s[0, 0, m] for m in range(TILES)]
    blocks = [block_s[0, 0, m] for m in range(TILES)]
    live = count_s[0, 0]

    def earlier(which):
        for m in range(TILES):
            rows = slice(m * 128, (m + 1) * 128)
            at = jnp.minimum(sources[m], CHAIN - 2)
            total = None if 0 in which else old[m]
            for b in which:
                left = pt[b, rows, 0:ROWS] if b in (0, 8) else pt[b, rows]
                if b == 0:
                    right = gx[at, 0, 0:ROWS]
                elif b == 8:
                    right = gx[at, 0, ROWS : 2 * ROWS]
                else:
                    right = gx[at, b]
                term = dot(left, right)
                total = term if total is None else total + term
            old[m] = total

    mine = lax.rem(y, 2) * SIDE + x
    columns = pl.ds(pl.multiple_of(mine * 128, 128), 128)

    def spread(src, dst, send, recv):
        return [
            pltpu.make_async_remote_copy(
                src_ref=src, dst_ref=dst.at[mine], send_sem=send.at[i], recv_sem=recv.at[mine],
                device_id={"leaf": other}, device_id_type=pl.DeviceIdType.MESH,
            )
            for i, other in enumerate(near)
        ]

    def arrive(src, dst, send, recv):
        for i, other in enumerate(near):
            pltpu.make_async_remote_copy(
                src_ref=src, dst_ref=dst.at[i], send_sem=send.at[i], recv_sem=recv.at[i],
                device_id={"leaf": other}, device_id_type=pl.DeviceIdType.MESH,
            ).wait_recv()

    def side_dots(i, which):
        total = None if 0 in which else tacc[...]
        for b in which:
            left = pd[i, b, :, 0:ROWS] if b in (0, 8) else pd[i, b]
            term = dot(left, chunk(gb, b))
            total = term if total is None else total + term
        tacc[...] = total

    t_args = (tacc, tfull, t_send, t_recv)
    w_args = (tacc, wfull, w_send, w_recv)

    def window_0a():
        prepare(0, 1)

    def window_0b():
        for load in loads[2:]:
            load.wait()
        gb[0, 0:ROWS] = jnp.where(core == 0, suba[0, :, columns], dinva[0, :, columns])
        send_own(9)
        prepare(2)

    def window_1a():
        pass_on(9, (1,))
        prepare(3, 4)

    def window_1b():
        pass_on(9, (2,))
        prepare(5)
        prepare_tile(0)

    def window_2a():
        pass_on(9, (3,))
        prepare(6)
        prepare_tile(1)

    def window_2b():
        pass_on(9, (4,))
        store_pairs(7, turned(dinva[1]))

    def window_3a():
        pass_on(9, (5,))
        prepare_tile(2)

    def window_3b():
        pass_on(9, (6,))

        @pl.when(core == 0)
        def _():
            side_dots(7, range(0, 6))

    def window_4a():
        pass_on(9, (7,))

        @pl.when(core == 0)
        def _():
            side_dots(7, range(6, 8))

    def window_4b():
        receive(9, 8)

        @pl.when(core == 0)
        def _():
            side_dots(7, range(8, 9))
            for copy in spread(*t_args):
                copy.start()

    def window_5b():
        @pl.when(core == 1)
        def _():
            arrive(*t_args)
            store_pairs(8, turned(jnp.concatenate([tfull[i] for i in range(8)], axis=1)))
            side_dots(8, range(0, 2))

    def window_6a():
        earlier(range(0, 3))

        @pl.when(core == 1)
        def _():
            side_dots(8, range(2, 5))

    def window_6b():
        earlier(range(3, 6))

        @pl.when(core == 1)
        def _():
            side_dots(8, range(5, 9))
            for copy in spread(*w_args):
                copy.start()

    def window_7a():
        earlier(range(6, 9))
        place_rhs()

    windows = [
        (window_0a, window_0b), (window_1a, window_1b), (window_2a, window_2b), (window_3a, window_3b),
        (window_4a, window_4b), (None, window_5b), (window_6a, window_6b),
    ]

    loads[0].wait()
    loads[1].wait()
    for s in range(CHAIN):
        k = 2 * s
        total, consume = multiply(k, k)
        gather(k, consume, *windows[k])
        solved = total[0]
        buffer(k + 1)[0, 0:ROWS] = solved
        out_local[0, s] = solved
        if s + 1 < CHAIN:
            total, consume = multiply(k + 1, k + 1)
            gather(k + 1, consume, *windows[k + 1])
            buffer(k + 2)[0, 0:ROWS] = rhs[0, s + 1] - total[0]

    half = lax.rem(me, 2)
    home = lax.div(me, 2)
    lane = lax.broadcasted_iota(jnp.int32, (8, 128), 1)
    sub_at = lax.broadcasted_iota(jnp.int32, (8, 128), 0)
    inside = jnp.logical_and(lax.div(lane, ROWS) == half, lax.div(sub_at, 4) == core)
    def place_rhs():
        for a in range(2):
            prow[0:4, 0:ROWS] = rhs_anc[a]
            quad = prow[0:8]
            wide = jnp.where(sub_at < 4, quad, pltpu.roll(quad, 4, axis=0))
            wide = jnp.where(lane < ROWS, wide, pltpu.roll(wide, ROWS, axis=1))
            give[a] = jnp.where(inside, wide, 0.0)

    last = []

    def consume_last(b):
        left = pt[b, :, 0:ROWS] if b in (0, 8) else pt[b]
        term = dot(left, chunk(gl, b))
        if last:
            last[0] = last[0] + term
        else:
            last.append(term)

    gather(7, consume_last, window_7a)
    for m in range(TILES):
        term = jnp.where(sources[m] == CHAIN - 1, last[0][m * 128 : (m + 1) * 128], old[m])
        term = jnp.where(m < live, term, 0.0)
        cells[m] = jnp.transpose(term).reshape(N, 8, 128)

    def build(role, out):
        for d in range(SIDE):
            for e in range(SIDE):
                xx = jnp.where(role == 0, lax.rem(x + d, SIDE), lax.rem(x + e, SIDE))
                yy = jnp.where(role == 0, lax.rem(y + e, SIDE), lax.rem(y + d, SIDE))
                cell = yy * SIDE + xx
                pieces = [cells[m, cell] for m in range(TILES)]
                for b in range(8):
                    value = jnp.zeros((8, 128), F32)
                    for m in range(TILES):
                        value = value - jnp.where(blocks[m] == role * 8 + b, pieces[m], 0.0)
                    if d == 0 and e == 0:
                        value = value + jnp.where(home == b, give[role], 0.0)
                    out[d, e, b] = value

    def remote(src, dst, send, recv, **where):
        return pltpu.make_async_remote_copy(
            src_ref=src, dst_ref=dst, send_sem=send, recv_sem=recv, device_id=where, device_id_type=pl.DeviceIdType.MESH
        )

    build(1 - core, theirs)
    pairs = [remote(theirs.at[d], pool.at[d], pair_send.at[d], pair_recv.at[d], leaf=partner) for d in range(SIDE)]
    for d in (2, 1, 3, 0):
        pairs[d].start()
    build(core, mid)
    ones = [None] + [
        remote(mid.at[d], inbox1.at[d - 1], one_send.at[d - 1], one_recv.at[d - 1], leaf=one_of[d]) for d in range(1, SIDE)
    ]
    for d in (2, 1, 3, 0):
        pairs[d].wait_recv()
        mid[d] = mid[d] + pool[d]
        if d:
            ones[d].start()
    for d in (1, 3, 2):
        ones[d].wait_recv()
    zbuf[...] = mid[0] + inbox1[0] + inbox1[1] + inbox1[2]
    twos = [None] + [
        remote(zbuf.at[d], inbox2.at[d - 1], two_send.at[d - 1], two_recv.at[d - 1], leaf=two_of[d]) for d in range(1, SIDE)
    ]
    for d in (2, 1, 3):
        twos[d].start()
    for d in (1, 3, 2):
        twos[d].wait_recv()
    gz[0, 0:ROWS] = (zbuf[0] + inbox2[0] + inbox2[1] + inbox2[2]).reshape(ROWS, RHS)

    sums = []

    def add_up(b):
        piece = chunk(gz, b)
        if b not in (0, 8):
            piece = piece[0:ROWS] + piece[ROWS : 2 * ROWS]
        if sums:
            sums[0] = sums[0] + piece
        else:
            sums.append(piece)

    gather(8, add_up)
    wanted = sums[0]
    first = jnp.zeros((8, ROWS), F32)
    for b in range(8):
        first = first + dot_nt(wanted[b * 8 : b * 8 + 8], dinva[core, :, b * 128 : (b + 1) * 128])

    def swap(src, dst, i):
        return remote(src, dst, swap_send.at[i], swap_recv.at[i], leaf=partner)

    def down():
        return swap(swap_out, swap_in, 0)

    def back():
        return swap(swap_out.at[1], swap_in.at[1], 1)

    @pl.when(core == 0)
    def _():
        arrive(*w_args)
        second = jnp.zeros((8, ROWS), F32)
        for b in range(8):
            second = second + dot_nt(wanted[b * 8 : b * 8 + 8], wfull[b])
        swap_out[0, :, 0:ROWS] = first
        swap_out[1, :, 0:ROWS] = second
        down().start()
        back().wait_recv()
        for a in range(2):
            out_anc[a] = (swap_out[0] if a == 0 else swap_in[1])[0:4, 0:ROWS]
        down().wait_send()
        for copy in spread(*t_args):
            copy.wait_send()

    @pl.when(core == 1)
    def _():
        down().wait_recv()
        swap_out[1, :, 0:ROWS] = first - swap_in[1, :, 0:ROWS]
        back().start()
        for a in range(2):
            out_anc[a] = (swap_in[0] if a == 0 else swap_out[1])[4:8, 0:ROWS]
        back().wait_send()
        for copy in spread(*w_args):
            copy.wait_send()

    for k in range(10):
        finish(k)
    for d in range(SIDE):
        pairs[d].wait_send()
        if d:
            ones[d].wait_send()
            twos[d].wait_send()


def on_device(rhs_local, diag_inv_local, sub_local, tiles, tile_block, tile_source, tile_count, rhs_anc, diag_inv_anc, sub_anc):
    vmem = pl.BlockSpec(memory_space=pltpu.VMEM)
    smem = pl.BlockSpec(memory_space=pltpu.SMEM)
    hbm = pl.BlockSpec(memory_space=pl.ANY)
    dma = pltpu.SemaphoreType.DMA
    local, anc = pl.pallas_call(
        kernel,
        out_shape=(
            jax.ShapeDtypeStruct((1, CHAIN, ROWS, RHS), F32),
            jax.ShapeDtypeStruct((2, 4, ROWS), F32),
        ),
        in_specs=[smem, smem, smem, vmem, vmem, hbm, hbm, hbm, hbm, hbm],
        out_specs=(vmem, vmem),
        scratch_shapes=[
            pltpu.VMEM((4, ROWS, 1024), F32),
            pltpu.VMEM((3, ROWS, 1024), F32),
            pltpu.VMEM((TILES, 128, 1024), F32),
            pltpu.VMEM((2, ROWS, 1024), F32),
            pltpu.VMEM((1, ROWS, 1024), F32),
            pltpu.VMEM((9, SLOTS, ROWS, 128), F32),
            pltpu.VMEM((SLOTS, TILES * 128, 128), F32),
            pltpu.VMEM((4, 8, 128, RHS), F32),
            pltpu.VMEM((3, 8, 128, RHS), F32),
            pltpu.VMEM((8, 128, RHS), F32),
            pltpu.VMEM((8, 128, RHS), F32),
            pltpu.VMEM((TILES, 128, RHS), F32),
            pltpu.VMEM((TILES, N, 8, 128), F32),
            pltpu.VMEM((SIDE, SIDE, 8, 8, 128), F32),
            pltpu.VMEM((SIDE, SIDE, 8, 8, 128), F32),
            pltpu.VMEM((3, SIDE, 8, 8, 128), F32),
            pltpu.VMEM((SIDE, SIDE, 8, 8, 128), F32),
            pltpu.VMEM((3, 8, 8, 128), F32),
            pltpu.VMEM((SIDE, 8, 8, 128), F32),
            pltpu.VMEM((8, 128, RHS), F32),
            pltpu.VMEM((ROWS, 128), F32),
            pltpu.VMEM((8, ROWS, 128), F32),
            pltpu.VMEM((8, ROWS, 128), F32),
            pltpu.VMEM((2, 8, 128), F32),
            pltpu.VMEM((2, 8, 128), F32),
            pltpu.VMEM((2, 8, 128), F32),
            pltpu.VMEM((8, 128), F32),
            dma((5,)),
            dma((10, 2, 8, PIECES)),
            dma((10, 2, 8, PIECES)),
            dma((SIDE,)),
            dma((SIDE,)),
            dma((3,)),
            dma((3,)),
            dma((3,)),
            dma((3,)),
            dma((8,)),
            dma((8,)),
            dma((8,)),
            dma((8,)),
            dma((2,)),
            dma((2,)),
        ],
        compiler_params=pltpu.CompilerParams(
            collective_id=0, has_side_effects=True, vmem_limit_bytes=56 * 1024 * 1024
        ),
    )(tile_block, tile_source, tile_count, rhs_local, jnp.transpose(rhs_anc, (0, 2, 1)), diag_inv_local, sub_local, tiles, diag_inv_anc, sub_anc)
    return local, jnp.transpose(anc, (0, 2, 1))


def solution(mesh):
    return jax.shard_map(
        on_device,
        mesh=mesh,
        in_specs=(
            P("leaf", None, "grp", None),
            P("leaf", None, "grp", None),
            P("leaf", None, "grp", None),
            P("leaf", "grp", None, None, None),
            P("leaf", "grp", None),
            P("leaf", "grp", None),
            P("leaf", "grp"),
            P(None, "grp", "leaf"),
            P(None, "grp", None),
            P(None, "grp", None),
        ),
        out_specs=(P("leaf", None, "grp", None), P(None, "grp", "leaf")),
        check_vma=False,
    )
```

time: 195 us -> 166 us (0.85); the launches traced: 191 us -> 165 us
  Pallas kernels: 186 us -> 161 us
    pallas_call x1, Pallas kernels: 186 us -> 161 us  [on_device(): pl.pallas_call(kernel, out_shape=(jax.ShapeDtypeStruct((1, CHAIN, ROWS, R...]
where the time goes in v2:
time: 166 us; the launch traced here: 165 us
  Pallas kernels  161 us (97%)
  local copies, waits for them, and re-layouts  2.85 us (2%)
    pallas_call x1, Pallas kernels, on_device(): pl.pallas_call(kernel, out_shape=(jax.ShapeDtypeStruct((1, CHAIN, ROWS, R...  161 us

profile of v2, /device:TPU:6, one launch (start us, length us, event | category | flops | bytes accessed | tf_op | source)
XLA Modules:
  0.0 164.7 jit_solution(17806966478691675378)
XLA Ops:
  1.3 160.6 %shard_map.113 = (f32[1,4,64,128]{3,2,1,0:T(8,128)}, f32[2,4,64]{2,1,0:T(4,128)}) custom-call(s32[1,1,3]{2,1,0:T(1,128)} %block_s.1, s32[1,1,3]{2,1,0:T(1,128)} %source_s.1, s32[1,1]{1,0:T(1,128)S(6)} %copy.14.count_s, f32[1,4,64,128]{3,2,1,0:T(8,128)} %rhs.1, f32[2,4,64]{2,1,0:T(4,128)} %bitcast.3, f32[1,4,64,1024]{3,2,1,0:T(8,128)} %dinv_h.1, ...), custom_call_target="tpu_custom_call" | custom-call | tf_op jit(solution)/shard_map/pallas_call | solution.py:514
  161.9 1.6 copy.15
  163.5 1.3 copy.16

commit v3 on v2

--- a/solution.py
+++ b/solution.py
@@ -15,10 +15,10 @@
 TILES = 3
 SLOTS = 9
 
-CHILDREN = {0: (5, 2, 1), 2: (3,), 5: (8, 7, 6, 4)}
-RELAYS = ((5, 2),)
-EARLY = (1, 2, 5)
-LATE = (3, 6, 4, 7, 8)
+CHILDREN = {0: (5, 1), 1: (2,), 2: (3,), 5: (8, 7, 6, 4)}
+RELAYS = ((1,), (5,), (2,))
+EARLY = (1,)
+LATE = (6, 4, 3, 7, 8)
 RING = {i: (i + 1,) for i in range(8)}
 PIECES = 2
 EDGES = sorted({abs(b - a) for tree in (CHILDREN, RING) for a, bs in tree.items() for b in bs})

time: 166 us -> 166 us (level); the launches traced: 165 us -> 163 us
  Pallas kernels: 161 us -> 159 us
    pallas_call x1, Pallas kernels: 161 us -> 159 us  [on_device(): pl.pallas_call(kernel, out_shape=(jax.ShapeDtypeStruct((1, CHAIN, ROWS, R...]
where the time goes in v3:
time: 166 us; the launch traced here: 163 us
  Pallas kernels  159 us (96%)
  local copies, waits for them, and re-layouts  2.85 us (2%)
    pallas_call x1, Pallas kernels, on_device(): pl.pallas_call(kernel, out_shape=(jax.ShapeDtypeStruct((1, CHAIN, ROWS, R...  159 us

profile of v3, /device:TPU:6, one launch (start us, length us, event | category | flops | bytes accessed | tf_op | source)
XLA Modules:
  0.0 162.7 jit_solution(5241739390674828804)
XLA Ops:
  1.3 158.6 %shard_map.113 = (f32[1,4,64,128]{3,2,1,0:T(8,128)}, f32[2,4,64]{2,1,0:T(4,128)}) custom-call(s32[1,1,3]{2,1,0:T(1,128)} %block_s.1, s32[1,1,3]{2,1,0:T(1,128)} %source_s.1, s32[1,1]{1,0:T(1,128)S(6)} %copy.14.count_s, f32[1,4,64,128]{3,2,1,0:T(8,128)} %rhs.1, f32[2,4,64]{2,1,0:T(4,128)} %bitcast.3, f32[1,4,64,1024]{3,2,1,0:T(8,128)} %dinv_h.1, ...), custom_call_target="tpu_custom_call" | custom-call | tf_op jit(solution)/shard_map/pallas_call | solution.py:514
  159.9 1.6 copy.15
  161.4 1.3 copy.16
